TPU v7x, 256 devices: a whole 4x4x8 slice. The times are simulated.
256 devices in a mesh: tm: 8 (over y, core), space: 32 (over x, z).
Axes of the slice: x: 4, y: 4, z: 8, core: 2. Of those that a mesh axis runs over, the one named last changes fastest.
Arguments:
- snapshots: float32 [2048, 128, 1024], P('space', None, 'tm'), may hold values from -6 to 6
- land_mask: int32 [2048, 128], P('space'), may hold values 0 or 1
- taps_rows: float32 [6], replicated, may hold values from -2.5 to 2.5
- taps_cols: float32 [6], replicated, may hold values from -2.5 to 2.5
- probes: float32 [1024, 64, 128], P('space'), may hold values from -6 to 6
Outputs:
- basis: float32 [1024, 64, 128], P('space', None, 'tm')
- coefficients: float32 [128, 128], P('tm')
All inputs are finite; a program needn't handle non-finite values. No bound on the sum of `land_mask` on one device may be relied on, other than what follows from the above.
Results may differ from a plain program's by a relative error of at most 0.00028.
Values sent between devices are 32-bit elements; how exact they have to be, the bound alone decides.
A program may use at most 64 MiB of HBM per device.

v0:
```python
import jax
import jax.numpy as jnp
from jax import lax
from jax.sharding import PartitionSpec as P

SIGN_STEPS = 8
exact_dot = lax.Precision.HIGHEST


def padded_2(x, sides, width):
    for axis, dim in sides:
        size, length = (lax.axis_size(axis), x.shape[dim])
        up = [(i, (i + 1) % size) for i in range(size - 1)]
        down = [(j, i) for i, j in up]
        last = lax.slice_in_dim(x, length - width, length, axis=dim)
        initial = lax.slice_in_dim(x, 0, width, axis=dim)
        before = lax.ppermute(last, axis, up)
        after = lax.ppermute(initial, axis, down)
        x = jnp.concatenate([before, x, after], axis=dim)
    return x


def partner(block, axis, distance):
    count = lax.axis_size(axis)
    route = []
    for low in range(count):
        high = low | 1 << distance
        if high != low and high < count:
            route += [(low, high), (high, low)]
    return lax.ppermute(block, axis, route)


def band_matrix(tap_values, out_count, in_width, shift_by):
    row_ids = lax.broadcasted_iota(jnp.int32, (out_count, in_width), 0)
    col_ids = lax.broadcasted_iota(jnp.int32, (out_count, in_width), 1)
    tap_offset = col_ids - 2 * row_ids - shift_by
    band_table = jnp.zeros((out_count, in_width), jnp.float32)
    for tap_index in range(6):
        band_table = band_table + jnp.where(tap_offset == tap_index, tap_values[tap_index], 0.0)
    return band_table


def merge_level(paired):
    partial_gram = jnp.einsum("gra,grb->gab", paired, paired, precision=exact_dot)
    gram_total = lax.psum(partial_gram, "space")
    order_size = gram_total.shape[-1]
    identity = jnp.eye(order_size, dtype=jnp.float32)
    mean_eig = jnp.sum(gram_total * identity, axis=(1, 2)) / order_size
    shifted = gram_total - mean_eig[:, None, None] * identity
    norm_scale = jnp.sqrt(jnp.sum(shifted * shifted, axis=(1, 2)) + 1e-06)
    sign_iter = shifted / norm_scale[:, None, None]
    for sweep_index in range(SIGN_STEPS):
        square = jnp.einsum("gab,gbc->gac", sign_iter, sign_iter, precision=exact_dot)
        sign_iter = 1.5 * sign_iter - 0.5 * jnp.einsum(
            "gab,gbc->gac", sign_iter, square, precision=exact_dot
        )
    projector = 0.5 * (identity + sign_iter)
    half_order = order_size // 2
    combine = projector[:, :, :half_order] + projector[:, :, half_order:]
    return jnp.einsum("gra,gab->grb", paired, combine, precision=exact_dot)


def local(snapshots, land_mask, taps_rows, taps_cols, probes):
    rows_dev, cell_cols, columns = snapshots.shape
    ocean_field = snapshots * land_mask.astype(jnp.float32)[:, :, None]
    across = band_matrix(taps_cols, cell_cols // 2, cell_cols, -2)
    narrowed = jnp.einsum("jy,xys->xjs", across, ocean_field, precision=exact_dot)
    padded = padded_2(narrowed, (("space", 0),), 3)
    row_filter = band_matrix(taps_rows, rows_dev // 2, rows_dev + 6, 1)
    filtered = jnp.einsum("ip,pjs->ijs", row_filter, padded, precision=exact_dot)
    cell_rows = rows_dev // 2 * (cell_cols // 2)
    factor = filtered.reshape(cell_rows, columns)
    flat_probes = probes.reshape(cell_rows, probes.shape[2])
    levels = lax.axis_size("tm").bit_length() - 1
    position = lax.axis_index("tm")
    merged = factor
    for level_index in range(levels):
        partner_fac = partner(merged, "tm", level_index)
        is_upper = position >> level_index & 1 == 1
        lower_part = jnp.where(is_upper, partner_fac, merged)
        upper_part = jnp.where(is_upper, merged, partner_fac)
        merged = merge_level(jnp.concatenate([lower_part, upper_part], axis=1)[None])[0]
    width_dev = columns // lax.axis_size("tm")
    col_start = position * width_dev
    partial_coef = jnp.einsum("rs,rp->sp", merged, flat_probes, precision=exact_dot)
    coefficients = lax.psum(partial_coef, "space")
    basis_own = lax.dynamic_slice_in_dim(merged, col_start, width_dev, 1)
    coef_own = lax.dynamic_slice_in_dim(coefficients, col_start, width_dev, 0)
    return (basis_own.reshape(rows_dev // 2, cell_cols // 2, width_dev), coef_own)


def solution(mesh):
    placed = (P("space", None, "tm"), P("space", None), P(), P(), P("space", None, None))
    return jax.shard_map(
        local,
        mesh=mesh,
        in_specs=placed,
        out_specs=(P("space", None, "tm"), P("tm", None)),
        check_vma=False,
    )
```

profile of v0, /device:TPU:2, one launch (start us, length us, event | category | flops | bytes accessed | tf_op | source)
XLA Modules:
  0.0 723.5 jit_solution(15306966266729676532)
XLA Ops:
  9.5 9.0 %fusion.11 = f32[64,64,128]{2,1,0:T(8,128)S(1)} fusion(f32[64,128,128]{2,1,0:T(8,128)} %param.5, f32[64,128]{1,0:T(8,128)S(1)} %convert_element_type.22, f32[]{:T(128)} %bitcast.12, f32[]{:T(128)} %bitcast.11, f32[]{:T(128)} %bitcast.10, f32[]{:T(128)} %bitcast.9, f32[]{:T(128)} %bitcast.8, f32[]{:T(128)} %bitcast.7, s32[64]{0:T(128)S(1)} %iota_multiply_fusion), kind=kOutput, calls=%fused_computation.15 | convolution fusion | flops 806510592 | bytes 6324504 | tf_op jit(solution)/shard_map/jy,xys->xjs/dot_general | solution.py:67
  18.6 3.8 collective-permute-start
  22.4 5.8 collective-permute-start.1
  30.8 6.5 fusion.2
  38.9 1.9 collective-permute-done.2
  40.7 1.7 broadcast_select_fusion.1
  42.4 4.2 fusion.14
  47.1 145.3 %all-reduce.5.cloned.1.call-done = f32[1,256,256]{2,1,0:T(8,128)} async-done(((f32[1,256,256]{2,1,0:T(8,128)}), f32[1,256,256]{2,1,0:T(8,128)}) %all-reduce.5.cloned.1.call-update) | async-done | bytes 262160 | tf_op jit(solution)/shard_map/psum | solution.py:45
  194.6 1.6 multiply_reduce_fusion.2
  205.3 3.3 fusion.9
  210.1 19.3 %collective-permute-done.3 = f32[2048,128]{0,1:T(8,128)} collective-permute-done((f32[2048,128]{0,1:T(8,128)}, f32[2048,128]{0,1:T(8,128)}, u32[]{:S(2)}, u32[]{:S(2)}) %collective-permute-start.3) | collective-permute-done | bytes 1048608 | tf_op jit(solution)/shard_map/ppermute | solution.py:30
  229.4 1.7 broadcast_select_fusion.3
  231.1 2.6 fusion.15
  233.9 141.9 %all-reduce.7.cloned.1.call-done = f32[1,256,256]{2,1,0:T(8,128)} async-done(((f32[1,256,256]{2,1,0:T(8,128)}), f32[1,256,256]{2,1,0:T(8,128)}) %all-reduce.7.cloned.1.call-update) | async-done | bytes 262160 | tf_op jit(solution)/shard_map/psum | solution.py:45
  378.0 1.6 multiply_reduce_fusion.1
  388.7 2.3 fusion.7
  391.0 3.0 collective-permute-start.4
  394.0 19.3 %collective-permute-done.4 = f32[2048,128]{0,1:T(8,128)} collective-permute-done((f32[2048,128]{0,1:T(8,128)}, f32[2048,128]{0,1:T(8,128)}, u32[]{:S(2)}, u32[]{:S(2)}) %collective-permute-start.4) | collective-permute-done | bytes 1048608 | tf_op jit(solution)/shard_map/ppermute | solution.py:30
  413.3 1.7 broadcast_select_fusion.5
  415.0 2.6 fusion.16
  417.9 141.8 %all-reduce.9.cloned.1.call-done = f32[1,256,256]{2,1,0:T(8,128)} async-done(((f32[1,256,256]{2,1,0:T(8,128)}), f32[1,256,256]{2,1,0:T(8,128)}) %all-reduce.9.cloned.1.call-update) | async-done | bytes 262160 | tf_op jit(solution)/shard_map/psum | solution.py:45
  562.0 1.6 multiply_reduce_fusion
  574.0 1.8 fusion.268
  576.8 138.7 %all-reduce.11.cloned.1.call-done = f32[128,128]{1,0:T(8,128)} async-done(((f32[128,128]{1,0:T(8,128)}), f32[128,128]{1,0:T(8,128)}) %all-reduce.11.cloned.1.call-update) | async-done | bytes 65552 | tf_op jit(solution)/shard_map/psum | solution.py:86
  (86 shorter events, 42.0 us)
Async XLA Ops:
  7.2 566.8 %copy-start = (f32[32,64,128]{2,1,0:T(8,128)S(1)}, f32[32,64,128]{2,1,0:T(8,128)}, u32[]{:S(2)}) copy-start(f32[32,64,128]{2,1,0:T(8,128)} %param.9) | copy-start | bytes 3145732
  7.2 185.2 %all-reduce.5.cloned.1.call-start = ((), (), s32[]{:S(2)}) async-start(), calls=%async_computation | async-start | bytes 524288 | tf_op jit(solution)/shard_map/psum | solution.py:45
  9.5 18.7 %copy-start.4 = (f32[6]{0:T(128)S(1)}, f32[6]{0:T(128)}, u32[]{:S(2)}) copy-start(f32[6]{0:T(128)} %param.7) | copy-start | bytes 76
  18.6 10.5 %collective-permute-start = (f32[3,64,128]{2,1,0:T(8,128)S(1)}, f32[3,64,128]{2,1,0:T(8,128)S(1)}, u32[]{:S(2)}, u32[]{:S(2)}) collective-permute-start(f32[3,64,128]{2,1,0:T(8,128)S(1)} %get-tuple-element.10), channel_id=1, source_target_pairs={{0,1},{1,2},{2,3},{3,4},{4,5},{5,6},{6,7},{7,8},{8,9},{9,10},{10,1... | collective-permute-start | bytes 294920 | tf_op jit(solution)/shard_map/ppermute | solution.py:17
  22.4 8.0 %collective-permute-start.1 = (f32[3,64,128]{2,1,0:T(8,128)S(1)}, f32[3,64,128]{2,1,0:T(8,128)S(1)}, u32[]{:S(2)}, u32[]{:S(2)}) collective-permute-start(f32[3,64,128]{2,1,0:T(8,128)S(1)} %get-tuple-element.11), channel_id=1, source_target_pairs={{1,0},{2,1},{3,2},{4,3},{5,4},{6,5},{7,6},{8,7},{9,8},{10,9},{11,1... | collective-permute-start | bytes 294920 | tf_op jit(solution)/shard_map/ppermute | solution.py:18
  37.8 1.0 copy-start.3
  37.9 2.9 collective-permute-start.2
  46.6 329.2 %all-reduce.7.cloned.1.call-start = ((), (), s32[]{:S(2)}) async-start(), calls=%async_computation.1 | async-start | bytes 524288 | tf_op jit(solution)/shard_map/psum | solution.py:45
  208.6 20.8 %collective-permute-start.3 = (f32[2048,128]{0,1:T(8,128)}, f32[2048,128]{0,1:T(8,128)}, u32[]{:S(2)}, u32[]{:S(2)}) collective-permute-start(f32[2048,128]{0,1:T(8,128)} %fusion.9), channel_id=1, source_target_pairs={{0,64},{64,0},{32,96},{96,32},{128,192},{192,128},{160,224},{224,1... | collective-permute-start | bytes 3145736 | tf_op jit(solution)/shard_map/ppermute | solution.py:30
  233.7 326.0 %all-reduce.9.cloned.1.call-start = ((), (), s32[]{:S(2)}) async-start(), calls=%async_computation.2 | async-start | bytes 524288 | tf_op jit(solution)/shard_map/psum | solution.py:45
  391.0 22.3 %collective-permute-start.4 = (f32[2048,128]{0,1:T(8,128)}, f32[2048,128]{0,1:T(8,128)}, u32[]{:S(2)}, u32[]{:S(2)}) collective-permute-start(f32[2048,128]{0,1:T(8,128)} %fusion.7), channel_id=1, source_target_pairs={{0,128},{128,0},{32,160},{160,32},{64,192},{192,64},{96,224},{224,... | collective-permute-start | bytes 3145736 | tf_op jit(solution)/shard_map/ppermute | solution.py:30
  415.0 150.7 %copy-start.1 = (f32[2048,128]{0,1:T(8,128)}, f32[2048,128]{0,1:T(8,128)S(1)}, u32[]{:S(2)}) copy-start(f32[2048,128]{0,1:T(8,128)S(1)} %get-tuple-element.5) | copy-start | bytes 3145732
  417.6 297.8 %all-reduce.11.cloned.1.call-start = ((), (), s32[]{:S(2)}) async-start(), calls=%async_computation.3 | async-start | bytes 131072 | tf_op jit(solution)/shard_map/psum | solution.py:86
  570.3 2.4 copy-start.2
Sparse Core Ops, SparseCore 0:
  46.7 145.6 all-reduce.4
  233.8 141.9 all-reduce.6
  417.7 141.9 all-reduce.8
  575.9 139.4 all-reduce.10
where the time goes:
time: 731 us; the launch traced here: 724 us
  waiting for transfers between devices  610 us (83%)
  matrix products  58.2 us (8%)
  between operations  18.6 us (3%)
  other arithmetic  15.7 us (2%)
  starting transfers between devices  15.3 us (2%)
    psum x3, waiting for transfers between devices, merge_level(): gram_total = lax.psum(partial_gram, 'space')  429 us
    psum x1, waiting for transfers between devices, local(): coefficients = lax.psum(partial_coef, 'space')  139 us
    ppermute x3, waiting for transfers between devices, partner(): return lax.ppermute(block, axis, route)  40.4 us
  transfers between devices with their start and end apart: 9, of which 9 were waited for; matrix products, arithmetic and copies ran while one was open for 0% of the time, Pallas kernels for 0%

commit v1 on v0

--- a/solution.py
+++ b/solution.py
@@ -5,6 +5,15 @@
 
 SIGN_STEPS = 8
 exact_dot = lax.Precision.HIGHEST
+
+
+def doubling_sum(value, axis):
+    peers = lax.axis_size(axis)
+    total, stride = (value, 1)
+    while stride < peers:
+        total = total + lax.ppermute(total, axis, [(i, i ^ stride) for i in range(peers)])
+        stride = 2 * stride
+    return total
 
 
 def padded_2(x, sides, width):
@@ -42,7 +51,7 @@
 
 def merge_level(paired):
     partial_gram = jnp.einsum("gra,grb->gab", paired, paired, precision=exact_dot)
-    gram_total = lax.psum(partial_gram, "space")
+    gram_total = doubling_sum(partial_gram, "space")
     order_size = gram_total.shape[-1]
     identity = jnp.eye(order_size, dtype=jnp.float32)
     mean_eig = jnp.sum(gram_total * identity, axis=(1, 2)) / order_size

time: 731 us -> 459 us (0.63)
  waiting for transfers between devices: 610 us -> 328 us
  starting transfers between devices: 15.3 us -> 36.8 us
  matrix products: 58.2 us -> 49.9 us
    psum x3 -> x0, waiting for transfers between devices: 429 us -> none  [merge_level(): gram_total = lax.psum(partial_gram, 'space')]
    ppermute x0 -> x15, waiting for transfers between devices: none -> 140 us  [doubling_sum(): lax.ppermute(total, axis, [(i, i ^ stride) for i in range(peers)])]
    ppermute x0 -> x15, starting transfers between devices: none -> 22.3 us  [doubling_sum(): lax.ppermute(total, axis, [(i, i ^ stride) for i in range(peers)])]
  transfers between devices with their start and end apart: 9 -> 21, of which waited for: 9 -> 21; matrix products, arithmetic and copies ran while one was open for 0% -> 0% of each run, Pallas kernels for 0% -> 0%
where the time goes in v1:
time: 459 us; the launch traced here: 450 us
  waiting for transfers between devices  328 us (71%)
  matrix products  49.9 us (11%)
  starting transfers between devices  36.8 us (8%)
  between operations  19 us (4%)
  other arithmetic  10.1 us (2%)
  local copies, waits for them, and re-layouts  6.03 us (1%)
    ppermute x15, waiting for transfers between devices, doubling_sum(): lax.ppermute(total, axis, [(i, i ^ stride) for i in range(peers)])  140 us
    psum x1, waiting for transfers between devices, local(): coefficients = lax.psum(partial_coef, 'space')  140 us
    ppermute x3, waiting for transfers between devices, partner(): return lax.ppermute(block, axis, route)  45.9 us
    ppermute x15, starting transfers between devices, doubling_sum(): lax.ppermute(total, axis, [(i, i ^ stride) for i in range(peers)])  22.3 us
    dot_general x24, matrix products, merge_level(): jnp.einsum('gab,gbc->gac', sign_iter, square, precision=exact_dot)  9.25 us
  transfers between devices with their start and end apart: 21, of which 21 were waited for; matrix products, arithmetic and copies ran while one was open for 0% of the time, Pallas kernels for 0%

profile of v1, /device:TPU:2, one launch (start us, length us, event | category | flops | bytes accessed | tf_op | source)
XLA Modules:
  0.0 449.8 jit_solution(5661989173621370735)
XLA Ops:
  9.6 9.1 %fusion.11 = f32[64,64,128]{2,1,0:T(8,128)S(1)} fusion(f32[64,128,128]{2,1,0:T(8,128)} %param.5, f32[64,128]{1,0:T(8,128)S(1)} %convert_element_type.22, f32[]{:T(128)} %bitcast.12, f32[]{:T(128)} %bitcast.11, f32[]{:T(128)} %bitcast.10, f32[]{:T(128)} %bitcast.9, f32[]{:T(128)} %bitcast.8, f32[]{:T(128)} %bitcast.7, s32[64]{0:T(128)S(1)} %iota_multiply_fusion), kind=kOutput, calls=%fused_computation.15 | convolution fusion | flops 806510592 | bytes 6324504 | tf_op jit(solution)/shard_map/jy,xys->xjs/dot_general | solution.py:76
  18.7 3.8 collective-permute-start
  22.5 5.8 %collective-permute-start.1 = (f32[3,64,128]{2,1,0:T(8,128)S(1)}, f32[3,64,128]{2,1,0:T(8,128)S(1)}, u32[]{:S(2)}, u32[]{:S(2)}) collective-permute-start(f32[3,64,128]{2,1,0:T(8,128)S(1)} %get-tuple-element.17), channel_id=1, source_target_pairs={{1,0},{2,1},{3,2},{4,3},{5,4},{6,5},{7,6},{8,7},{9,8},{10,9},{11,1... | collective-permute-start | bytes 294920 | tf_op jit(solution)/shard_map/ppermute | solution.py:27
  30.8 6.5 %fusion.2 = f32[32,64,128]{2,0,1:T(8,128)S(1)} fusion(f32[70,64,128]{2,1,0:T(8,128)S(1)} %pad_maximum_fusion, f32[]{:T(128)} %bitcast.5, f32[]{:T(128)} %bitcast.4, f32[]{:T(128)} %bitcast.3, f32[]{:T(128)} %bitcast.2, f32[]{:T(128)} %bitcast.1, f32[]{:T(128)} %bitcast, s32[32]{0:T(128)S(1)} %iota_multiply_fusion.1), kind=kOutput, calls=%fused_computation.2 | convolution fusion | flops 220243520 | bytes 3342488 | tf_op jit(solution)/shard_map/ip,pjs->ijs/dot_general | solution.py:79
  42.5 3.5 fusion.14
  46.5 8.0 %collective-permute-done.3 = f32[1,256,256]{2,1,0:T(8,128)S(1)} collective-permute-done((f32[1,256,256]{2,1,0:T(8,128)S(1)}, f32[1,256,256]{2,1,0:T(8,128)S(1)}, u32[]{:S(2)}, u32[]{:S(2)}) %collective-permute-start.3) | collective-permute-done | bytes 262176 | tf_op jit(solution)/shard_map/ppermute | solution.py:14
  54.5 4.4 collective-permute-start.4
  58.9 11.6 %collective-permute-done.4 = f32[1,256,256]{2,1,0:T(8,128)S(1)} collective-permute-done((f32[1,256,256]{2,1,0:T(8,128)S(1)}, f32[1,256,256]{2,1,0:T(8,128)S(1)}, u32[]{:S(2)}, u32[]{:S(2)}) %collective-permute-start.4) | collective-permute-done | bytes 262176 | tf_op jit(solution)/shard_map/ppermute | solution.py:14
  73.5 13.9 %collective-permute-done.5 = f32[1,256,256]{2,1,0:T(8,128)S(1)} collective-permute-done((f32[1,256,256]{2,1,0:T(8,128)S(1)}, f32[1,256,256]{2,1,0:T(8,128)S(1)}, u32[]{:S(2)}, u32[]{:S(2)}) %collective-permute-start.5) | collective-permute-done | bytes 262176 | tf_op jit(solution)/shard_map/ppermute | solution.py:14
  88.0 7.7 %collective-permute-done.6 = f32[1,256,256]{2,1,0:T(8,128)S(1)} collective-permute-done((f32[1,256,256]{2,1,0:T(8,128)S(1)}, f32[1,256,256]{2,1,0:T(8,128)S(1)}, u32[]{:S(2)}, u32[]{:S(2)}) %collective-permute-start.6) | collective-permute-done | bytes 262176 | tf_op jit(solution)/shard_map/ppermute | solution.py:14
  98.4 6.8 %collective-permute-done.7 = f32[1,256,256]{2,1,0:T(8,128)S(1)} collective-permute-done((f32[1,256,256]{2,1,0:T(8,128)S(1)}, f32[1,256,256]{2,1,0:T(8,128)S(1)}, u32[]{:S(2)}, u32[]{:S(2)}) %collective-permute-start.7) | collective-permute-done | bytes 262176 | tf_op jit(solution)/shard_map/ppermute | solution.py:14
  119.0 22.1 %collective-permute-done.8 = f32[2048,128]{0,1:T(8,128)} collective-permute-done((f32[2048,128]{0,1:T(8,128)}, f32[2048,128]{0,1:T(8,128)}, u32[]{:S(2)}, u32[]{:S(2)}) %collective-permute-start.8) | collective-permute-done | bytes 1048608 | tf_op jit(solution)/shard_map/ppermute | solution.py:39
  144.8 6.4 %collective-permute-done.9 = f32[1,256,256]{2,1,0:T(8,128)S(1)} collective-permute-done((f32[1,256,256]{2,1,0:T(8,128)S(1)}, f32[1,256,256]{2,1,0:T(8,128)S(1)}, u32[]{:S(2)}, u32[]{:S(2)}) %collective-permute-start.9) | collective-permute-done | bytes 262176 | tf_op jit(solution)/shard_map/ppermute | solution.py:14
  154.0 8.4 %collective-permute-done.10 = f32[1,256,256]{2,1,0:T(8,128)S(1)} collective-permute-done((f32[1,256,256]{2,1,0:T(8,128)S(1)}, f32[1,256,256]{2,1,0:T(8,128)S(1)}, u32[]{:S(2)}, u32[]{:S(2)}) %collective-permute-start.10) | collective-permute-done | bytes 262176 | tf_op jit(solution)/shard_map/ppermute | solution.py:14
  165.3 13.0 %collective-permute-done.11 = f32[1,256,256]{2,1,0:T(8,128)S(1)} collective-permute-done((f32[1,256,256]{2,1,0:T(8,128)S(1)}, f32[1,256,256]{2,1,0:T(8,128)S(1)}, u32[]{:S(2)}, u32[]{:S(2)}) %collective-permute-start.11) | collective-permute-done | bytes 262176 | tf_op jit(solution)/shard_map/ppermute | solution.py:14
  178.9 7.7 %collective-permute-done.12 = f32[1,256,256]{2,1,0:T(8,128)S(1)} collective-permute-done((f32[1,256,256]{2,1,0:T(8,128)S(1)}, f32[1,256,256]{2,1,0:T(8,128)S(1)}, u32[]{:S(2)}, u32[]{:S(2)}) %collective-permute-start.12) | collective-permute-done | bytes 262176 | tf_op jit(solution)/shard_map/ppermute | solution.py:14
  188.8 6.8 %collective-permute-done.13 = f32[1,256,256]{2,1,0:T(8,128)S(1)} collective-permute-done((f32[1,256,256]{2,1,0:T(8,128)S(1)}, f32[1,256,256]{2,1,0:T(8,128)S(1)}, u32[]{:S(2)}, u32[]{:S(2)}) %collective-permute-start.13) | collective-permute-done | bytes 262176 | tf_op jit(solution)/shard_map/ppermute | solution.py:14
  210.0 21.9 %collective-permute-done.14 = f32[2048,128]{0,1:T(8,128)S(1)} collective-permute-done((f32[2048,128]{0,1:T(8,128)}, f32[2048,128]{0,1:T(8,128)S(1)}, u32[]{:S(2)}, u32[]{:S(2)}) %collective-permute-start.14) | collective-permute-done | bytes 1048608 | tf_op jit(solution)/shard_map/ppermute | solution.py:39
  235.3 6.4 %collective-permute-done.15 = f32[1,256,256]{2,1,0:T(8,128)S(1)} collective-permute-done((f32[1,256,256]{2,1,0:T(8,128)S(1)}, f32[1,256,256]{2,1,0:T(8,128)S(1)}, u32[]{:S(2)}, u32[]{:S(2)}) %collective-permute-start.15) | collective-permute-done | bytes 262176 | tf_op jit(solution)/shard_map/ppermute | solution.py:14
  242.0 21.3 %collective-permute-done.16 = f32[1,256,256]{2,1,0:T(8,128)S(1)} collective-permute-done((f32[1,256,256]{2,1,0:T(8,128)S(1)}, f32[1,256,256]{2,1,0:T(8,128)S(1)}, u32[]{:S(2)}, u32[]{:S(2)}) %collective-permute-start.16) | collective-permute-done | bytes 262176 | tf_op jit(solution)/shard_map/ppermute | solution.py:14
  263.4 10.3 %collective-permute-done.17 = f32[1,256,256]{2,1,0:T(8,128)S(1)} collective-permute-done((f32[1,256,256]{2,1,0:T(8,128)S(1)}, f32[1,256,256]{2,1,0:T(8,128)S(1)}, u32[]{:S(2)}, u32[]{:S(2)}) %collective-permute-start.17) | collective-permute-done | bytes 262176 | tf_op jit(solution)/shard_map/ppermute | solution.py:14
  274.2 5.9 %collective-permute-done.18 = f32[1,256,256]{2,1,0:T(8,128)S(1)} collective-permute-done((f32[1,256,256]{2,1,0:T(8,128)S(1)}, f32[1,256,256]{2,1,0:T(8,128)S(1)}, u32[]{:S(2)}, u32[]{:S(2)}) %collective-permute-start.18) | collective-permute-done | bytes 262176 | tf_op jit(solution)/shard_map/ppermute | solution.py:14
  282.0 6.2 %collective-permute-done.19 = f32[1,256,256]{2,1,0:T(8,128)S(1)} collective-permute-done((f32[1,256,256]{2,1,0:T(8,128)S(1)}, f32[1,256,256]{2,1,0:T(8,128)S(1)}, u32[]{:S(2)}, u32[]{:S(2)}) %collective-permute-start.19) | collective-permute-done | bytes 262176 | tf_op jit(solution)/shard_map/ppermute | solution.py:14
  301.2 140.2 %all-reduce.2.cloned.1.call-done = f32[128,128]{1,0:T(8,128)} async-done(((f32[128,128]{1,0:T(8,128)}), f32[128,128]{1,0:T(8,128)}) %all-reduce.2.cloned.1.call-update) | async-done | bytes 65552 | tf_op jit(solution)/shard_map/psum | solution.py:95
  (119 shorter events, 73.1 us)
Async XLA Ops:
  7.2 291.3 %copy-start = (f32[32,64,128]{2,1,0:T(8,128)S(1)}, f32[32,64,128]{2,1,0:T(8,128)}, u32[]{:S(2)}) copy-start(f32[32,64,128]{2,1,0:T(8,128)} %param.9) | copy-start | bytes 3145732
  7.2 434.2 %all-reduce.2.cloned.1.call-start = ((), (), s32[]{:S(2)}) async-start(), calls=%async_computation | async-start | bytes 131072 | tf_op jit(solution)/shard_map/psum | solution.py:95
  9.5 18.8 %copy-start.4 = (f32[6]{0:T(128)S(1)}, f32[6]{0:T(128)}, u32[]{:S(2)}) copy-start(f32[6]{0:T(128)} %param.7) | copy-start | bytes 76
  18.7 10.5 %collective-permute-start = (f32[3,64,128]{2,1,0:T(8,128)S(1)}, f32[3,64,128]{2,1,0:T(8,128)S(1)}, u32[]{:S(2)}, u32[]{:S(2)}) collective-permute-start(f32[3,64,128]{2,1,0:T(8,128)S(1)} %get-tuple-element.16), channel_id=1, source_target_pairs={{0,1},{1,2},{2,3},{3,4},{4,5},{5,6},{6,7},{7,8},{8,9},{9,10},{10,1... | collective-permute-start | bytes 294920 | tf_op jit(solution)/shard_map/ppermute | solution.py:26
  22.5 8.0 %collective-permute-start.1 = (f32[3,64,128]{2,1,0:T(8,128)S(1)}, f32[3,64,128]{2,1,0:T(8,128)S(1)}, u32[]{:S(2)}, u32[]{:S(2)}) collective-permute-start(f32[3,64,128]{2,1,0:T(8,128)S(1)} %get-tuple-element.17), channel_id=1, source_target_pairs={{1,0},{2,1},{3,2},{4,3},{5,4},{6,5},{7,6},{8,7},{9,8},{10,9},{11,1... | collective-permute-start | bytes 294920 | tf_op jit(solution)/shard_map/ppermute | solution.py:27
  37.9 2.9 collective-permute-start.2
  46.0 8.4 %collective-permute-start.3 = (f32[1,256,256]{2,1,0:T(8,128)S(1)}, f32[1,256,256]{2,1,0:T(8,128)S(1)}, u32[]{:S(2)}, u32[]{:S(2)}) collective-permute-start(f32[1,256,256]{2,1,0:T(8,128)S(1)} %fusion.14), channel_id=1, source_target_pairs={{0,1},{1,0},{2,3},{3,2},{4,5},{5,4},{6,7},{7,6},{8,9},{9,8},{10,11... | collective-permute-start | bytes 786440 | tf_op jit(solution)/shard_map/ppermute | solution.py:14
  54.5 16.1 %collective-permute-start.4 = (f32[1,256,256]{2,1,0:T(8,128)S(1)}, f32[1,256,256]{2,1,0:T(8,128)S(1)}, u32[]{:S(2)}, u32[]{:S(2)}) collective-permute-start(f32[1,256,256]{2,1,0:T(8,128)S(1)} %add.123), channel_id=1, source_target_pairs={{0,2},{1,3},{2,0},{3,1},{4,6},{5,7},{6,4},{7,5},{8,10},{9,11},{10,... | collective-permute-start | bytes 786440 | tf_op jit(solution)/shard_map/ppermute | solution.py:14
  70.6 16.8 %collective-permute-start.5 = (f32[1,256,256]{2,1,0:T(8,128)S(1)}, f32[1,256,256]{2,1,0:T(8,128)S(1)}, u32[]{:S(2)}, u32[]{:S(2)}) collective-permute-start(f32[1,256,256]{2,1,0:T(8,128)S(1)} %add.124), channel_id=1, source_target_pairs={{0,4},{1,5},{2,6},{3,7},{4,0},{5,1},{6,2},{7,3},{8,12},{9,13},{10,... | collective-permute-start | bytes 786440 | tf_op jit(solution)/shard_map/ppermute | solution.py:14
  87.4 8.3 %collective-permute-start.6 = (f32[1,256,256]{2,1,0:T(8,128)S(1)}, f32[1,256,256]{2,1,0:T(8,128)S(1)}, u32[]{:S(2)}, u32[]{:S(2)}) collective-permute-start(f32[1,256,256]{2,1,0:T(8,128)S(1)} %add.125), channel_id=1, source_target_pairs={{0,8},{1,9},{2,10},{3,11},{4,12},{5,13},{6,14},{7,15},{8,0},{9,1},... | collective-permute-start | bytes 786440 | tf_op jit(solution)/shard_map/ppermute | solution.py:14
  95.8 9.4 %collective-permute-start.7 = (f32[1,256,256]{2,1,0:T(8,128)S(1)}, f32[1,256,256]{2,1,0:T(8,128)S(1)}, u32[]{:S(2)}, u32[]{:S(2)}) collective-permute-start(f32[1,256,256]{2,1,0:T(8,128)S(1)} %add.126), channel_id=1, source_target_pairs={{0,16},{1,17},{2,18},{3,19},{4,20},{5,21},{6,22},{7,23},{8,24},{9,... | collective-permute-start | bytes 786440 | tf_op jit(solution)/shard_map/ppermute | solution.py:14
  117.4 23.7 %collective-permute-start.8 = (f32[2048,128]{0,1:T(8,128)}, f32[2048,128]{0,1:T(8,128)}, u32[]{:S(2)}, u32[]{:S(2)}) collective-permute-start(f32[2048,128]{0,1:T(8,128)} %fusion.9), channel_id=1, source_target_pairs={{0,64},{64,0},{32,96},{96,32},{128,192},{192,128},{160,224},{224,1... | collective-permute-start | bytes 3145736 | tf_op jit(solution)/shard_map/ppermute | solution.py:39
  144.7 6.5 %collective-permute-start.9 = (f32[1,256,256]{2,1,0:T(8,128)S(1)}, f32[1,256,256]{2,1,0:T(8,128)S(1)}, u32[]{:S(2)}, u32[]{:S(2)}) collective-permute-start(f32[1,256,256]{2,1,0:T(8,128)S(1)} %fusion.15), channel_id=1, source_target_pairs={{0,1},{1,0},{2,3},{3,2},{4,5},{5,4},{6,7},{7,6},{8,9},{9,8},{10,11... | collective-permute-start | bytes 786440 | tf_op jit(solution)/shard_map/ppermute | solution.py:14
  151.2 11.2 %collective-permute-start.10 = (f32[1,256,256]{2,1,0:T(8,128)S(1)}, f32[1,256,256]{2,1,0:T(8,128)S(1)}, u32[]{:S(2)}, u32[]{:S(2)}) collective-permute-start(f32[1,256,256]{2,1,0:T(8,128)S(1)} %add.131), channel_id=1, source_target_pairs={{0,2},{1,3},{2,0},{3,1},{4,6},{5,7},{6,4},{7,5},{8,10},{9,11},{10,... | collective-permute-start | bytes 786440 | tf_op jit(solution)/shard_map/ppermute | solution.py:14
  162.4 15.9 %collective-permute-start.11 = (f32[1,256,256]{2,1,0:T(8,128)S(1)}, f32[1,256,256]{2,1,0:T(8,128)S(1)}, u32[]{:S(2)}, u32[]{:S(2)}) collective-permute-start(f32[1,256,256]{2,1,0:T(8,128)S(1)} %add.132), channel_id=1, source_target_pairs={{0,4},{1,5},{2,6},{3,7},{4,0},{5,1},{6,2},{7,3},{8,12},{9,13},{10,... | collective-permute-start | bytes 786440 | tf_op jit(solution)/shard_map/ppermute | solution.py:14
  178.3 8.3 %collective-permute-start.12 = (f32[1,256,256]{2,1,0:T(8,128)S(1)}, f32[1,256,256]{2,1,0:T(8,128)S(1)}, u32[]{:S(2)}, u32[]{:S(2)}) collective-permute-start(f32[1,256,256]{2,1,0:T(8,128)S(1)} %add.133), channel_id=1, source_target_pairs={{0,8},{1,9},{2,10},{3,11},{4,12},{5,13},{6,14},{7,15},{8,0},{9,1},... | collective-permute-start | bytes 786440 | tf_op jit(solution)/shard_map/ppermute | solution.py:14
  186.7 9.0 %collective-permute-start.13 = (f32[1,256,256]{2,1,0:T(8,128)S(1)}, f32[1,256,256]{2,1,0:T(8,128)S(1)}, u32[]{:S(2)}, u32[]{:S(2)}) collective-permute-start(f32[1,256,256]{2,1,0:T(8,128)S(1)} %add.134), channel_id=1, source_target_pairs={{0,16},{1,17},{2,18},{3,19},{4,20},{5,21},{6,22},{7,23},{8,24},{9,... | collective-permute-start | bytes 786440 | tf_op jit(solution)/shard_map/ppermute | solution.py:14
  206.9 25.1 %collective-permute-start.14 = (f32[2048,128]{0,1:T(8,128)}, f32[2048,128]{0,1:T(8,128)S(1)}, u32[]{:S(2)}, u32[]{:S(2)}) collective-permute-start(f32[2048,128]{0,1:T(8,128)} %fusion.7), channel_id=1, source_target_pairs={{0,128},{128,0},{32,160},{160,32},{64,192},{192,64},{96,224},{224,... | collective-permute-start | bytes 3145736 | tf_op jit(solution)/shard_map/ppermute | solution.py:39
  233.3 40.4 %copy-start.1 = (f32[2048,128]{0,1:T(8,128)}, f32[2048,128]{0,1:T(8,128)S(1)}, u32[]{:S(2)}) copy-start(f32[2048,128]{0,1:T(8,128)S(1)} %get-tuple-element.11) | copy-start | bytes 3145732
  235.2 6.5 %collective-permute-start.15 = (f32[1,256,256]{2,1,0:T(8,128)S(1)}, f32[1,256,256]{2,1,0:T(8,128)S(1)}, u32[]{:S(2)}, u32[]{:S(2)}) collective-permute-start(f32[1,256,256]{2,1,0:T(8,128)S(1)} %fusion.16), channel_id=1, source_target_pairs={{0,1},{1,0},{2,3},{3,2},{4,5},{5,4},{6,7},{7,6},{8,9},{9,8},{10,11... | collective-permute-start | bytes 786440 | tf_op jit(solution)/shard_map/ppermute | solution.py:14
  241.7 21.6 %collective-permute-start.16 = (f32[1,256,256]{2,1,0:T(8,128)S(1)}, f32[1,256,256]{2,1,0:T(8,128)S(1)}, u32[]{:S(2)}, u32[]{:S(2)}) collective-permute-start(f32[1,256,256]{2,1,0:T(8,128)S(1)} %add.139), channel_id=1, source_target_pairs={{0,2},{1,3},{2,0},{3,1},{4,6},{5,7},{6,4},{7,5},{8,10},{9,11},{10,... | collective-permute-start | bytes 786440 | tf_op jit(solution)/shard_map/ppermute | solution.py:14
  263.3 10.4 %collective-permute-start.17 = (f32[1,256,256]{2,1,0:T(8,128)S(1)}, f32[1,256,256]{2,1,0:T(8,128)S(1)}, u32[]{:S(2)}, u32[]{:S(2)}) collective-permute-start(f32[1,256,256]{2,1,0:T(8,128)S(1)} %add.140), channel_id=1, source_target_pairs={{0,4},{1,5},{2,6},{3,7},{4,0},{5,1},{6,2},{7,3},{8,12},{9,13},{10,... | collective-permute-start | bytes 786440 | tf_op jit(solution)/shard_map/ppermute | solution.py:14
  273.7 6.5 %collective-permute-start.18 = (f32[1,256,256]{2,1,0:T(8,128)S(1)}, f32[1,256,256]{2,1,0:T(8,128)S(1)}, u32[]{:S(2)}, u32[]{:S(2)}) collective-permute-start(f32[1,256,256]{2,1,0:T(8,128)S(1)} %add.141), channel_id=1, source_target_pairs={{0,8},{1,9},{2,10},{3,11},{4,12},{5,13},{6,14},{7,15},{8,0},{9,1},... | collective-permute-start | bytes 786440 | tf_op jit(solution)/shard_map/ppermute | solution.py:14
  280.2 8.0 %collective-permute-start.19 = (f32[1,256,256]{2,1,0:T(8,128)S(1)}, f32[1,256,256]{2,1,0:T(8,128)S(1)}, u32[]{:S(2)}, u32[]{:S(2)}) collective-permute-start(f32[1,256,256]{2,1,0:T(8,128)S(1)} %add.142), channel_id=1, source_target_pairs={{0,16},{1,17},{2,18},{3,19},{4,20},{5,21},{6,22},{7,23},{8,24},{9,... | collective-permute-start | bytes 786440 | tf_op jit(solution)/shard_map/ppermute | solution.py:14
  (2 other events, 3.3 us)
Sparse Core Ops, SparseCore 0:
  300.4 141.0 all-reduce.1
